TPU v7x, 32 devices: a whole 2x2x4 slice. The times are simulated.
32 devices in a mesh: groups: 2 (over x), rows: 16 (over z, y, core).
Axes of the slice: x: 2, y: 2, z: 4, core: 2. Of those that a mesh axis runs over, the one named last changes fastest.
Arguments:
- queries: bfloat16 [64, 4096], P(('groups', 'rows')), parts along dimension 0, may hold values from -128 to 128
- new_keys: bfloat16 [64, 4096], P(('groups', 'rows')), parts along dimension 0, may hold values from -4 to 4
- new_values: bfloat16 [64, 4096], P(('groups', 'rows')), parts along dimension 0, may hold values from -5 to 5
- cache_keys: bfloat16 [64, 64, 4096], P(('groups', 'rows')), parts along dimension 0, may hold values from -4 to 4
- cache_values: bfloat16 [64, 64, 4096], P(('groups', 'rows')), parts along dimension 0, may hold values from -5 to 5
- cache_lengths: int32 [64], P(('groups', 'rows')), parts along dimension 0, may hold values from 1 to 64, as said below
- out_weight: bfloat16 [4096, 4096], P('rows'), may hold values from -0.09375 to 0.09375
- codes: int32 [64, 768], P(('groups', 'rows')), parts along dimension 0, may hold values from 0 to 1073741823
- tile_slot: int32 [64], P(('groups', 'rows')), parts along dimension 0, may hold values from -1 to 3, as said below
- code_weight: float32 [5, 512], replicated, may hold values from -2.5 to 2.5
- conv_one: bfloat16 [3, 3, 512, 512], replicated, may hold values from -0.09375 to 0.09375
- conv_two: bfloat16 [3, 3, 512, 512], replicated, may hold values from -0.09375 to 0.09375
Outputs:
- mixed: bfloat16 [64, 4096], P(('groups', 'rows')), parts along dimension 0
- decoded: bfloat16 [256, 48, 512], P(('groups', 'rows')), parts along dimension 0
There are 2 independent parts, one for each index of `groups`. A program takes and returns all parts, laid end to end along the dimension named above; an argument that names none is the same for every part. Nothing has to cross between parts.
Inputs may be any that keep to these rules, and one draw needn't show every extreme that they name: `cache_lengths`: some row's length is exactly 64. `tile_slot`: each slot 0 to 3 belongs to exactly one row; all other rows hold -1.
All inputs are finite; a program needn't handle non-finite values.
Results may differ from a plain program's by a relative error of at most 0.0075.
Values may be sent and summed in bfloat16 or wider, within the bound.
A program may use at most 64 MiB of HBM per device.

v0:
```python
import math

import jax
import jax.numpy as jnp
from jax import lax
from jax.sharding import PartitionSpec as P

HEADS = 32
HEAD_DIM = 128
FSQ_DIMS = 5
IMG_SPLIT = 4
TILE_H = 8
IMG_W = 48


def extended_2(cells, sides, width):
    for axis, dim in sides:
        count = lax.axis_size(axis)
        head = lax.slice_in_dim(cells, 0, width, axis=dim)
        tail = lax.slice_in_dim(cells, cells.shape[dim] - width, cells.shape[dim], axis=dim)
        cells = jnp.concatenate(
            [
                lax.ppermute(tail, axis, [(i, (i + 1) % count) for i in range(count)]),
                cells,
                lax.ppermute(head, axis, [((i + 1) % count, i) for i in range(count)]),
            ],
            axis=dim,
        )
    return cells


def convolve(padded, weights):
    out_h = padded.shape[0] - 2
    out_w = padded.shape[1] - 2
    channels = padded.shape[2]
    summed = jnp.zeros((out_h * out_w, weights.shape[3]), jnp.float32)
    for row_step in range(3):
        for col_step in range(3):
            window = padded[row_step : row_step + out_h, col_step : col_step + out_w].reshape(
                out_h * out_w, channels
            )
            summed = summed + jnp.dot(
                window, weights[row_step, col_step], preferred_element_type=jnp.float32
            )
    return summed.reshape(out_h, out_w, weights.shape[3])


def unpack(words, code_weight):
    lower = words % 32768
    upper = words // 32768
    position_codes = jnp.stack([lower, upper], 1).reshape(-1)
    levels = jnp.stack([position_codes // 8**level % 8 for level in range(FSQ_DIMS)], 1)
    values = (2 * levels - 7).astype(jnp.float32) * 0.125
    return jnp.dot(
        values, code_weight, precision=lax.Precision.HIGHEST, preferred_element_type=jnp.float32
    )


def attend(queries, new_keys, new_values, cache_keys, cache_values, cache_lengths):
    count = queries.shape[0]
    factor = 1.0 / math.sqrt(HEAD_DIM)
    query_heads = queries.reshape(count, HEADS, HEAD_DIM)
    key_heads = cache_keys.reshape(count, -1, HEADS, HEAD_DIM)
    value_heads = cache_values.reshape(count, -1, HEADS, HEAD_DIM)
    scores = (
        jnp.einsum("rhd,rlhd->rhl", query_heads, key_heads, preferred_element_type=jnp.float32)
        * factor
    )
    own_score = (
        jnp.sum(
            query_heads.astype(jnp.float32)
            * new_keys.astype(jnp.float32).reshape(count, HEADS, HEAD_DIM),
            -1,
        )
        * factor
    )
    live = (
        jnp.arange(key_heads.shape[1], dtype=jnp.int32)[None, None, :]
        < cache_lengths[:, None, None]
    )
    scores = jnp.where(live, scores, jnp.float32(-1e30))
    highest = jnp.maximum(jnp.max(scores, -1), own_score)
    cache_exp = jnp.where(live, jnp.exp(scores - highest[..., None]), jnp.float32(0.0))
    own_exp = jnp.exp(own_score - highest)
    denom = jnp.sum(cache_exp, -1) + own_exp
    cache_weight = (cache_exp / denom[..., None]).astype(jnp.bfloat16)
    own_weight = (own_exp / denom).astype(jnp.bfloat16)
    attended = jnp.einsum(
        "rhl,rlhd->rhd", cache_weight, value_heads, preferred_element_type=jnp.float32
    )
    attended = attended + own_weight.astype(jnp.float32)[..., None] * new_values.astype(
        jnp.float32
    ).reshape(count, HEADS, HEAD_DIM)
    return attended.reshape(count, HEADS * HEAD_DIM).astype(jnp.bfloat16)


def clear_edges(field, depth, section):
    height = field.shape[0]
    line = jnp.arange(height, dtype=jnp.int32)[:, None, None]
    cleared = (line < depth) & (section == 0) | (line >= height - depth) & (
        section == IMG_SPLIT - 1
    )
    return jnp.where(cleared, jnp.zeros((), field.dtype), field)


def widen_columns(field):
    return jnp.pad(field, ((0, 0), (1, 1), (0, 0)))


def single_rim(tile, section):
    extended = extended_2(tile, (("rows", 0),), 1)
    return widen_columns(clear_edges(extended, 1, section))


def on_device(
    queries,
    new_keys,
    new_values,
    cache_keys,
    cache_values,
    cache_lengths,
    out_weight,
    codes,
    tile_slot,
    code_weight,
    conv_one,
    conv_two,
):
    attended = attend(queries, new_keys, new_values, cache_keys, cache_values, cache_lengths)
    feature_rows = lax.all_to_all(attended, "rows", split_axis=1, concat_axis=0, tiled=True)
    own_count = attended.shape[0]
    partial_value = jnp.dot(feature_rows, out_weight, preferred_element_type=jnp.float32)
    summed = lax.psum(partial_value, "rows")
    own_rows = lax.dynamic_slice_in_dim(summed, lax.axis_index("rows") * own_count, own_count, 0)
    mixed = own_rows.astype(jnp.bfloat16)
    tiles = lax.axis_size("rows")
    place = lax.axis_index("rows")
    tile_number = (place + IMG_SPLIT // 2) % tiles
    section = tile_number % IMG_SPLIT
    tile_words = TILE_H * IMG_W // 2
    sections = codes.reshape(own_count, IMG_SPLIT, tile_words)
    destined = (jnp.arange(tiles, dtype=jnp.int32) + IMG_SPLIT // 2) % tiles
    target_slot = destined // IMG_SPLIT
    target_section = destined % IMG_SPLIT
    spread = jnp.take(sections, target_section, axis=1)
    matches = tile_slot[:, None] == target_slot[None, :]
    outgoing = jnp.sum(jnp.where(matches[:, :, None], spread, 0), 0)
    incoming = lax.all_to_all(outgoing, "rows", split_axis=0, concat_axis=0, tiled=True)
    chosen = jnp.sum(incoming, 0)
    latent = unpack(chosen, code_weight).reshape(TILE_H, IMG_W, -1).astype(jnp.bfloat16)
    hidden = convolve(single_rim(latent, section), conv_one)
    activated = jax.nn.silu(hidden).astype(jnp.bfloat16)
    decoded = convolve(single_rim(activated, section), conv_two).astype(jnp.bfloat16)
    return (mixed, decoded)


def solution(mesh):
    in_specs = (
        P(("groups", "rows"), None),
        P(("groups", "rows"), None),
        P(("groups", "rows"), None),
        P(("groups", "rows"), None, None),
        P(("groups", "rows"), None, None),
        P(("groups", "rows")),
        P("rows", None),
        P(("groups", "rows"), None),
        P(("groups", "rows")),
        P(),
        P(),
        P(),
    )
    out_specs = (P(("groups", "rows"), None), P(("groups", "rows"), None, None))
    return jax.shard_map(
        on_device, mesh=mesh, in_specs=in_specs, out_specs=out_specs, check_vma=False
    )
```

profile of v0, /device:TPU:0, one launch (start us, length us, event | category | flops | bytes accessed | tf_op | source)
XLA Modules:
  0.0 112.9 jit_solution(13891319534046034997)
XLA Ops:
  0.7 0.9 reshape.749
  1.6 0.6 gather_fusion
  2.2 0.7 broadcast_compare_fusion
  2.9 0.1 fusion.48
  3.1 0.6 all_to_all.21
  3.7 7.4 %all-to-all-start.1 = ((s32[16,1,192]{2,1,0:T(1,128)}), s32[16,1,192]{2,1,0:T(1,128)S(1)}, u32[]{:S(2)}, u32[]{:S(2)}) async-start(s32[16,1,192]{2,1,0:T(1,128)} %all_to_all.21), calls=%async_computation.1 | async-start | bytes 32768 | tf_op jit(solution)/shard_map/all_to_all | solution.py:148
  11.2 0.7 reshape.787
  11.9 0.7 iota_compare_fusion
  12.6 0.7 convert_bitcast_fusion.1
  13.4 1.9 %fusion.4 = f32[2,32,1,64]{3,2,1,0:T(1,128)S(1)} fusion(bf16[2,32,128,1]{2,3,1,0:T(2,128)(2,1)S(1)} %reshape.787, bf16[2,64,4096]{2,1,0:T(8,128)(2,1)} %param.15), kind=kOutput, calls=%fused_computation.22 | convolution fusion | flops 1048576 | bytes 1081344 | tf_op jit(solution)/shard_map/rhd,rlhd->rhl/dot_general | solution.py:66
  15.3 0.8 fusion.47
  16.1 0.2 fusion.51
  16.4 0.7 convert_bitcast_fusion
  17.2 1.6 %fusion.1 = f32[2,32,1,128]{3,2,1,0:T(1,128)S(1)} fusion(bf16[2,32,64,1]{2,1,0,3:T(8,128)(2,1)S(1)} %fusion.52, bf16[2,64,4096]{2,1,0:T(8,128)(2,1)} %param.16), kind=kOutput, calls=%fused_computation.19 | convolution fusion | flops 1048576 | bytes 1089536 | tf_op jit(solution)/shard_map/rhl,rlhd->rhd/dot_general | solution.py:88
  18.9 0.6 copy.21
  19.5 6.0 %all-to-all-start = ((bf16[2,16,256]{2,0,1:T(2,128)(2,1)}), bf16[2,16,256]{2,0,1:T(2,128)(2,1)S(1)}, u32[]{:S(2)}, u32[]{:S(2)}) async-start(bf16[2,16,256]{2,0,1:T(2,128)(2,1)} %copy.21), calls=%async_computation | async-start | bytes 32768 | tf_op jit(solution)/shard_map/all_to_all | solution.py:130
  25.6 0.1 copy.23
  25.7 0.1 reshape.750
  25.9 1.6 %convolution_convert_fusion = bf16[384,512]{1,0:T(8,128)(2,1)S(1)} fusion(f32[5,512]{1,0:T(8,128)} %param.21, s32[384,5]{0,1:T(8,128)S(1)} %stack.5), kind=kOutput, calls=%fused_computation.18 | convolution fusion | flops 12000768 | bytes 411136 | tf_op jit(solution)/shard_map/dot_general | solution.py:54
  27.5 0.5 collective-permute-start
  28.0 4.0 %collective-permute-start.1 = (bf16[1,48,512]{2,1,0:T(8,128)(2,1)S(1)}, bf16[1,48,512]{2,1,0:T(8,128)(2,1)S(1)}, u32[]{:S(2)}, u32[]{:S(2)}) collective-permute-start(bf16[1,48,512]{2,1,0:T(8,128)(2,1)S(1)} %get-tuple-element.25), channel_id=1, source_target_pairs={{1,0},{2,1},{3,2},{4,3},{5,4},{6,5},{7,6},{8,7},{9,8},{10,9},{11,1... | collective-permute-start | bytes 147464 | tf_op jit(solution)/shard_map/ppermute | solution.py:25
  32.1 0.5 fusion.74
  32.5 63.4 %all-reduce.3 = bf16[32,4096]{1,0:T(8,128)(2,1)S(1)} all-reduce(f32[32,4096]{1,0:T(8,128)S(1)} %fusion.74), channel_id=1, replica_groups=mesh['groups'=2,'rows'=16] {'rows'}, use_global_device_ids=true, to_apply=%region_3.4 | all-reduce | flops 131072 | bytes 786432 | tf_op jit(solution)/shard_map/psum | solution.py:133
  96.1 0.5 pad_slice_fusion.6
  96.6 1.7 %copy-done.1 = bf16[3,3,512,512]{3,2,1,0:T(8,128)(2,1)S(1)} copy-done((bf16[3,3,512,512]{3,2,1,0:T(8,128)(2,1)S(1)}, bf16[3,3,512,512]{3,2,1,0:T(8,128)(2,1)}, u32[]{:S(2)}) %copy-start.1) | copy-done | bytes 4718616
  98.3 0.4 fusion.25
  98.6 0.4 convolution_add_fusion.15
  99.0 0.4 convolution_add_fusion.14
  99.4 0.4 convolution_add_fusion.13
  99.7 0.4 convolution_add_fusion.12
  100.1 0.4 convolution_add_fusion.11
  100.5 0.4 convolution_add_fusion.10
  100.9 0.4 convolution_add_fusion.9
  101.3 0.4 convolution_add_fusion.8
  101.6 0.2 multiply_convert_fusion
  101.9 4.4 %collective-permute-start.3 = (bf16[1,48,512]{2,1,0:T(8,128)(2,1)S(1)}, bf16[1,48,512]{2,1,0:T(8,128)(2,1)S(1)}, u32[]{:S(2)}, u32[]{:S(2)}) collective-permute-start(bf16[1,48,512]{2,1,0:T(8,128)(2,1)S(1)} %get-tuple-element.23), channel_id=1, source_target_pairs={{1,0},{2,1},{3,2},{4,3},{5,4},{6,5},{7,6},{8,7},{9,8},{10,9},{11,1... | collective-permute-start | bytes 147464 | tf_op jit(solution)/shard_map/ppermute | solution.py:25
  106.4 0.6 dynamic-slice_convert_fusion
  107.0 1.1 %collective-permute-done.2 = bf16[1,48,512]{2,1,0:T(8,128)(2,1)S(1)} collective-permute-done((bf16[1,48,512]{2,1,0:T(8,128)(2,1)S(1)}, bf16[1,48,512]{2,1,0:T(8,128)(2,1)S(1)}, u32[]{:S(2)}, u32[]{:S(2)}) %collective-permute-start.2) | collective-permute-done | bytes 49184 | tf_op jit(solution)/shard_map/ppermute | solution.py:23
  108.3 0.5 pad_slice_fusion
  108.8 0.4 fusion.15
  109.2 0.4 convolution_add_fusion.7
  109.5 0.4 convolution_add_fusion.6
  109.9 0.4 convolution_add_fusion.5
  110.3 0.4 convolution_add_fusion.4
  110.7 0.4 convolution_add_fusion.3
  111.0 0.4 convolution_add_fusion.2
  111.4 0.4 convolution_add_fusion.1
  111.8 1.1 fusion
  (37 shorter events, 0.9 us)
Async XLA Ops:
  0.6 31.4 %copy-start = (bf16[256,4096]{1,0:T(8,128)(2,1)S(1)}, bf16[256,4096]{1,0:T(8,128)(2,1)}, u32[]{:S(2)}) copy-start(bf16[256,4096]{1,0:T(8,128)(2,1)} %param.18) | copy-start | bytes 6291460
  3.7 15.8 %all-to-all-start.1 = ((s32[16,1,192]{2,1,0:T(1,128)}), s32[16,1,192]{2,1,0:T(1,128)S(1)}, u32[]{:S(2)}, u32[]{:S(2)}) async-start(s32[16,1,192]{2,1,0:T(1,128)} %all_to_all.21), calls=%async_computation.1 | async-start | bytes 32768 | tf_op jit(solution)/shard_map/all_to_all | solution.py:148
  19.5 12.5 %all-to-all-start = ((bf16[2,16,256]{2,0,1:T(2,128)(2,1)}), bf16[2,16,256]{2,0,1:T(2,128)(2,1)S(1)}, u32[]{:S(2)}, u32[]{:S(2)}) async-start(bf16[2,16,256]{2,0,1:T(2,128)(2,1)} %copy.21), calls=%async_computation | async-start | bytes 32768 | tf_op jit(solution)/shard_map/all_to_all | solution.py:130
  27.5 68.4 %collective-permute-start = (bf16[1,48,512]{2,1,0:T(8,128)(2,1)S(1)}, bf16[1,48,512]{2,1,0:T(8,128)(2,1)S(1)}, u32[]{:S(2)}, u32[]{:S(2)}) collective-permute-start(bf16[1,48,512]{2,1,0:T(8,128)(2,1)S(1)} %get-tuple-element.24), channel_id=1, source_target_pairs={{0,1},{1,2},{2,3},{3,4},{4,5},{5,6},{6,7},{7,8},{8,9},{9,10},{10,1... | collective-permute-start | bytes 147464 | tf_op jit(solution)/shard_map/ppermute | solution.py:23
  28.0 68.0 %collective-permute-start.1 = (bf16[1,48,512]{2,1,0:T(8,128)(2,1)S(1)}, bf16[1,48,512]{2,1,0:T(8,128)(2,1)S(1)}, u32[]{:S(2)}, u32[]{:S(2)}) collective-permute-start(bf16[1,48,512]{2,1,0:T(8,128)(2,1)S(1)} %get-tuple-element.25), channel_id=1, source_target_pairs={{1,0},{2,1},{3,2},{4,3},{5,4},{6,5},{7,6},{8,7},{9,8},{10,9},{11,1... | collective-permute-start | bytes 147464 | tf_op jit(solution)/shard_map/ppermute | solution.py:25
  95.9 2.3 %copy-start.1 = (bf16[3,3,512,512]{3,2,1,0:T(8,128)(2,1)S(1)}, bf16[3,3,512,512]{3,2,1,0:T(8,128)(2,1)}, u32[]{:S(2)}) copy-start(bf16[3,3,512,512]{3,2,1,0:T(8,128)(2,1)} %param.22) | copy-start | bytes 14155780
  100.5 8.3 %slice-start = ((s8[4718592]{0:T(1024)(128)(4,1)}), s8[524288]{0:T(1024)(128)(4,1)S(1)}, s32[]{:S(2)}) async-start(s8[4718592]{0:T(1024)(128)(4,1)} %bitcast.146), calls=%async_computation.2 | async-start | bytes 1048576
  101.6 7.2 %slice-start.1 = ((s8[4718592]{0:T(1024)(128)(4,1)}), s8[4194304]{0:T(1024)(128)(4,1)S(1)}, s32[]{:S(2)}) async-start(s8[4718592]{0:T(1024)(128)(4,1)} %bitcast.146), calls=%async_computation.3 | async-start | bytes 8388608
  101.9 6.3 %collective-permute-start.2 = (bf16[1,48,512]{2,1,0:T(8,128)(2,1)S(1)}, bf16[1,48,512]{2,1,0:T(8,128)(2,1)S(1)}, u32[]{:S(2)}, u32[]{:S(2)}) collective-permute-start(bf16[1,48,512]{2,1,0:T(8,128)(2,1)S(1)} %get-tuple-element.22), channel_id=1, source_target_pairs={{0,1},{1,2},{2,3},{3,4},{4,5},{5,6},{6,7},{7,8},{8,9},{9,10},{10,1... | collective-permute-start | bytes 147464 | tf_op jit(solution)/shard_map/ppermute | solution.py:23
  101.9 6.2 %collective-permute-start.3 = (bf16[1,48,512]{2,1,0:T(8,128)(2,1)S(1)}, bf16[1,48,512]{2,1,0:T(8,128)(2,1)S(1)}, u32[]{:S(2)}, u32[]{:S(2)}) collective-permute-start(bf16[1,48,512]{2,1,0:T(8,128)(2,1)S(1)} %get-tuple-element.23), channel_id=1, source_target_pairs={{1,0},{2,1},{3,2},{4,3},{5,4},{6,5},{7,6},{8,7},{9,8},{10,9},{11,1... | collective-permute-start | bytes 147464 | tf_op jit(solution)/shard_map/ppermute | solution.py:25
where the time goes:
time: 114 us; the launch traced here: 113 us
  blocking collectives  63.4 us (56%)
  starting transfers between devices  22.4 us (20%)
  matrix products  12.8 us (11%)
  local copies, waits for them, and re-layouts  7.17 us (6%)
  other arithmetic  4.94 us (4%)
  waiting for transfers between devices  1.15 us (1%)
    psum x1, blocking collectives, on_device(): summed = lax.psum(partial_value, 'rows')  63.4 us
    ppermute x2, starting transfers between devices, extended_2(): lax.ppermute(head, axis, [((i + 1) % count, i) for i in range(count)])  8.47 us
    all_to_all x1, starting transfers between devices, on_device(): lax.all_to_all(outgoing, 'rows', split_axis=0, concat_axis=0, tiled=True)  7.41 us
    dot_general x18, matrix products, convolve(): jnp.dot(window, weights[row_step, col_step], preferred_element_type=jnp.f...  7.33 us
    all_to_all x1, starting transfers between devices, on_device(): lax.all_to_all(attended, 'rows', split_axis=1, concat_axis=0, tiled=True)  5.98 us
  transfers between devices with their start and end apart: 6, of which 1 were waited for; matrix products, arithmetic and copies ran while one was open for 10% of the time, Pallas kernels for 0%

commit v1 on v0

--- a/solution.py
+++ b/solution.py
@@ -11,22 +11,6 @@
 IMG_SPLIT = 4
 TILE_H = 8
 IMG_W = 48
-
-
-def extended_2(cells, sides, width):
-    for axis, dim in sides:
-        count = lax.axis_size(axis)
-        head = lax.slice_in_dim(cells, 0, width, axis=dim)
-        tail = lax.slice_in_dim(cells, cells.shape[dim] - width, cells.shape[dim], axis=dim)
-        cells = jnp.concatenate(
-            [
-                lax.ppermute(tail, axis, [(i, (i + 1) % count) for i in range(count)]),
-                cells,
-                lax.ppermute(head, axis, [((i + 1) % count, i) for i in range(count)]),
-            ],
-            axis=dim,
-        )
-    return cells
 
 
 def convolve(padded, weights):
@@ -107,11 +91,6 @@
     return jnp.pad(field, ((0, 0), (1, 1), (0, 0)))
 
 
-def single_rim(tile, section):
-    extended = extended_2(tile, (("rows", 0),), 1)
-    return widen_columns(clear_edges(extended, 1, section))
-
-
 def on_device(
     queries,
     new_keys,
@@ -130,15 +109,22 @@
     feature_rows = lax.all_to_all(attended, "rows", split_axis=1, concat_axis=0, tiled=True)
     own_count = attended.shape[0]
     partial_value = jnp.dot(feature_rows, out_weight, preferred_element_type=jnp.float32)
-    summed = lax.psum(partial_value, "rows")
-    own_rows = lax.dynamic_slice_in_dim(summed, lax.axis_index("rows") * own_count, own_count, 0)
-    mixed = own_rows.astype(jnp.bfloat16)
+    shares = lax.all_to_all(
+        partial_value.astype(jnp.bfloat16), "rows", split_axis=0, concat_axis=0, tiled=True
+    )
+    mixed = jnp.sum(
+        shares.reshape(-1, own_count, shares.shape[1]).astype(jnp.float32), 0
+    ).astype(jnp.bfloat16)
     tiles = lax.axis_size("rows")
     place = lax.axis_index("rows")
     tile_number = (place + IMG_SPLIT // 2) % tiles
     section = tile_number % IMG_SPLIT
     tile_words = TILE_H * IMG_W // 2
-    sections = codes.reshape(own_count, IMG_SPLIT, tile_words)
+    rim_words = 2 * IMG_W // 2
+    wide = jnp.pad(codes, ((0, 0), (rim_words, rim_words)))
+    sections = jnp.stack(
+        [wide[:, i * tile_words : (i + 1) * tile_words + 2 * rim_words] for i in range(IMG_SPLIT)], 1
+    )
     destined = (jnp.arange(tiles, dtype=jnp.int32) + IMG_SPLIT // 2) % tiles
     target_slot = destined // IMG_SPLIT
     target_section = destined % IMG_SPLIT
@@ -147,10 +133,12 @@
     outgoing = jnp.sum(jnp.where(matches[:, :, None], spread, 0), 0)
     incoming = lax.all_to_all(outgoing, "rows", split_axis=0, concat_axis=0, tiled=True)
     chosen = jnp.sum(incoming, 0)
-    latent = unpack(chosen, code_weight).reshape(TILE_H, IMG_W, -1).astype(jnp.bfloat16)
-    hidden = convolve(single_rim(latent, section), conv_one)
+    latent = unpack(chosen, code_weight).reshape(TILE_H + 4, IMG_W, -1).astype(jnp.bfloat16)
+    hidden = convolve(widen_columns(clear_edges(latent, 2, section)), conv_one)
     activated = jax.nn.silu(hidden).astype(jnp.bfloat16)
-    decoded = convolve(single_rim(activated, section), conv_two).astype(jnp.bfloat16)
+    decoded = convolve(widen_columns(clear_edges(activated, 1, section)), conv_two).astype(
+        jnp.bfloat16
+    )
     return (mixed, decoded)
 
 

time: 114 us -> 51.5 us (0.45)
  blocking collectives: 63.4 us -> 0 us
  starting transfers between devices: 22.4 us -> 14.4 us
  waiting for transfers between devices: 1.15 us -> 8.51 us
    psum x1 -> x0, blocking collectives: 63.4 us -> none  [on_device(): summed = lax.psum(partial_value, 'rows')]
    ppermute x4 -> x0, starting transfers between devices: 8.98 us -> none  [the longest x2 8.47 us: extended_2(): lax.ppermute(head, axis, [((i + 1) % count, i) for i in range(count)])]
    all_to_all x1, waiting for transfers between devices: 0.01 us -> 5.14 us  [on_device(): lax.all_to_all(outgoing, 'rows', split_axis=0, concat_axis=0, tiled=True)]
    all_to_all x1, starting transfers between devices: 7.41 us -> 3.5 us  [on_device(): lax.all_to_all(outgoing, 'rows', split_axis=0, concat_axis=0, tiled=True)]
    all_to_all x0 -> x1, starting transfers between devices: none -> 3.53 us  [on_device(): lax.all_to_all(partial_value.astype(jnp.bfloat16), 'rows', split_axis=0,...]
    all_to_all x1, waiting for transfers between devices: 0.01 us -> 3.37 us  [on_device(): lax.all_to_all(attended, 'rows', split_axis=1, concat_axis=0, tiled=True)]
    all_to_all x1, starting transfers between devices: 5.98 us -> 7.41 us  [on_device(): lax.all_to_all(attended, 'rows', split_axis=1, concat_axis=0, tiled=True)]
    ppermute x4 -> x0, waiting for transfers between devices: 1.15 us -> none  [the longest x2 1.14 us: extended_2(): lax.ppermute(tail, axis, [(i, (i + 1) % count) for i in range(count)])]
  transfers between devices with their start and end apart: 6 -> 3, of which waited for: 1 -> 2; matrix products, arithmetic and copies ran while one was open for 10% -> 28% of each run, Pallas kernels for 0% -> 0%
where the time goes in v1:
time: 51.5 us; the launch traced here: 50.6 us
  starting transfers between devices  14.4 us (28%)
  matrix products  13 us (25%)
  waiting for transfers between devices  8.51 us (17%)
  local copies, waits for them, and re-layouts  7.81 us (15%)
  other arithmetic  5.8 us (11%)
  between operations  1.04 us (2%)
    dot_general x18, matrix products, convolve(): jnp.dot(window, weights[row_step, col_step], preferred_element_type=jnp.f...  7.85 us
    all_to_all x1, starting transfers between devices, on_device(): lax.all_to_all(attended, 'rows', split_axis=1, concat_axis=0, tiled=True)  7.41 us
    all_to_all x1, waiting for transfers between devices, on_device(): lax.all_to_all(outgoing, 'rows', split_axis=0, concat_axis=0, tiled=True)  5.14 us
    all_to_all x1, starting transfers between devices, on_device(): lax.all_to_all(partial_value.astype(jnp.bfloat16), 'rows', split_axis=0,...  3.53 us
    all_to_all x1, starting transfers between devices, on_device(): lax.all_to_all(outgoing, 'rows', split_axis=0, concat_axis=0, tiled=True)  3.5 us
    all_to_all x1, waiting for transfers between devices, on_device(): lax.all_to_all(attended, 'rows', split_axis=1, concat_axis=0, tiled=True)  3.37 us
    dot_general x1, matrix products, attend(): jnp.einsum('rhd,rlhd->rhl', query_heads, key_heads, preferred_element_typ...  1.86 us
    unnamed x12, local copies, waits for them, and re-layouts  1.78 us
  transfers between devices with their start and end apart: 3, of which 2 were waited for; matrix products, arithmetic and copies ran while one was open for 28% of the time, Pallas kernels for 0%

profile of v1, /device:TPU:0, one launch (start us, length us, event | category | flops | bytes accessed | tf_op | source)
XLA Modules:
  0.0 50.6 jit_solution(16069184187874359425)
XLA Ops:
  0.7 0.9 %reshape.800 = bf16[2,32,128,1]{2,3,1,0:T(2,128)(2,1)S(1)} reshape(bf16[2,4096]{1,0:T(2,128)(2,1)} %param.12) | data formatting | bytes 32768 | tf_op jit(solution)/shard_map/reshape | solution.py:46
  1.5 0.7 %iota_compare_fusion = pred[2,64]{1,0:T(4,128)(4,1)S(1)} fusion(s32[2]{0:T(128)} %param.17), kind=kLoop, calls=%fused_computation.169 | loop fusion | flops 128 | bytes 136 | tf_op jit(solution)/shard_map/lt | solution.py:62
  2.3 0.7 %convert_bitcast_fusion.1 = f32[1,2,32,128]{3,1,2,0:T(2,128)S(1)} fusion(bf16[2,4096]{1,0:T(2,128)(2,1)} %param.13), kind=kLoop, calls=%fused_computation.88 | loop fusion | flops 8192 | bytes 49152
  3.0 1.9 %fusion.4 = f32[2,32,1,64]{3,2,1,0:T(1,128)S(1)} fusion(bf16[2,32,128,1]{2,3,1,0:T(2,128)(2,1)S(1)} %reshape.800, bf16[2,64,4096]{2,1,0:T(8,128)(2,1)} %param.15), kind=kOutput, calls=%fused_computation.23 | convolution fusion | flops 1048576 | bytes 1081344 | tf_op jit(solution)/shard_map/rhd,rlhd->rhl/dot_general | solution.py:50
  5.0 0.8 %fusion.49 = f32[2,32]{1,0:T(2,128)S(1)} fusion(f32[1,2,32,128]{3,1,2,0:T(2,128)S(1)} %convert_bitcast_fusion.1, bf16[1,2,32,128]{3,1,2,0:T(2,128)(2,1)} %bitcast.177), kind=kLoop, calls=%fused_computation.85 | loop fusion | flops 24512 | bytes 49408 | tf_op jit(solution)/shard_map/reduce_sum | solution.py:54
  5.8 0.2 fusion.52
  6.1 0.7 %convert_bitcast_fusion = f32[1,2,32,128]{3,1,2,0:T(2,128)S(1)} fusion(bf16[2,4096]{1,0:T(2,128)(2,1)} %param.14), kind=kLoop, calls=%fused_computation.87 | loop fusion | flops 8192 | bytes 49152
  6.8 1.7 %fusion.1 = f32[2,32,1,128]{3,2,1,0:T(1,128)S(1)} fusion(bf16[2,32,64,1]{2,1,0,3:T(8,128)(2,1)S(1)} %fusion.57, bf16[2,64,4096]{2,1,0:T(8,128)(2,1)} %param.16), kind=kOutput, calls=%fused_computation.20 | convolution fusion | flops 1048576 | bytes 1089536 | tf_op jit(solution)/shard_map/rhl,rlhd->rhd/dot_general | solution.py:72
  8.6 0.6 %copy.19 = bf16[2,16,256]{2,0,1:T(2,128)(2,1)} copy(bf16[2,16,256]{2,1,0:T(8,128)(2,1)S(1)} %convert_element_type.61) | data formatting | bytes 32768 | tf_op jit(solution)/shard_map/convert_element_type | solution.py:78
  9.2 7.4 %all-to-all-start = ((bf16[2,16,256]{2,0,1:T(2,128)(2,1)}), bf16[2,16,256]{2,0,1:T(2,128)(2,1)S(1)}, u32[]{:S(2)}, u32[]{:S(2)}) async-start(bf16[2,16,256]{2,0,1:T(2,128)(2,1)} %copy.19), calls=%async_computation | async-start | bytes 32768 | tf_op jit(solution)/shard_map/all_to_all | solution.py:109
  16.7 0.9 %fusion.61 = (s32[2,1,288]{2,0,1:T(2,128)S(1)}, s32[2,1,288]{2,0,1:T(2,128)S(1)}, s32[2,1,288]{2,0,1:T(2,128)S(1)}, s32[2,1,288]{2,0,1:T(2,128)S(1)}) fusion(s32[2,768]{1,0:T(2,128)} %param.19), kind=kLoop, calls=%fused_computation.138 | loop fusion | bytes 21504 | tf_op jit(solution)/shard_map/stack | solution.py:125
  17.6 0.6 %gather_fusion = s32[16,2,288]{2,1,0:T(2,128)S(1)} fusion(s32[2,4,288]{2,0,1:T(2,128)S(1)} %pad_add_fusion, s32[1024]{0:T(1024)S(1)} %pad_clamp_fusion), kind=kCustom, calls=%fused_computation | custom fusion | bytes 73792 | tf_op jit(solution)/shard_map/jit(_take)/gather | solution.py:131
  18.2 0.7 %broadcast_compare_fusion = pred[2,16]{0,1:T(8,128)(4,1)S(1)} fusion(s32[2]{0:T(128)} %param.20, s32[16]{0:T(128)S(1)} %and_select_fusion.14), kind=kLoop, calls=%fused_computation.125 | loop fusion | flops 32 | bytes 104 | tf_op jit(solution)/shard_map/eq | solution.py:132
  19.0 0.2 fusion.46
  19.2 0.6 %all_to_all.29 = s32[16,1,288]{2,1,0:T(1,128)} reshape(s32[16,288]{1,0:T(8,128)S(1)} %fusion.46) | data formatting | bytes 36864 | tf_op jit(solution)/shard_map/all_to_all | solution.py:134
  19.8 3.4 %all-to-all-done = bf16[2,16,256]{2,0,1:T(2,128)(2,1)S(1)} async-done(((bf16[2,16,256]{2,0,1:T(2,128)(2,1)}), bf16[2,16,256]{2,0,1:T(2,128)(2,1)S(1)}, u32[]{:S(2)}, u32[]{:S(2)}) %all-to-all-start) | async-done | bytes 16416 | tf_op jit(solution)/shard_map/all_to_all | solution.py:109
  23.1 3.5 %all-to-all-start.2 = ((s32[16,1,288]{2,1,0:T(1,128)}), s32[16,1,288]{2,1,0:T(1,128)S(1)}, u32[]{:S(2)}, u32[]{:S(2)}) async-start(s32[16,1,288]{2,1,0:T(1,128)} %all_to_all.29), calls=%async_computation.2 | async-start | bytes 49152 | tf_op jit(solution)/shard_map/all_to_all | solution.py:134
  26.7 0.5 convolution_convert_fusion
  27.2 0.9 %all_to_all.27 = bf16[16,2,4096]{2,1,0:T(2,128)(2,1)} reshape(bf16[32,4096]{1,0:T(8,128)(2,1)S(1)} %convolution_convert_fusion) | data formatting | bytes 524288 | tf_op jit(solution)/shard_map/all_to_all | solution.py:112
  28.0 5.1 %all-to-all-done.2 = s32[16,1,288]{2,1,0:T(1,128)S(1)} async-done(((s32[16,1,288]{2,1,0:T(1,128)}), s32[16,1,288]{2,1,0:T(1,128)S(1)}, u32[]{:S(2)}, u32[]{:S(2)}) %all-to-all-start.2) | async-done | bytes 18464 | tf_op jit(solution)/shard_map/all_to_all | solution.py:134
  33.2 3.5 %all-to-all-start.1 = ((bf16[16,2,4096]{2,1,0:T(2,128)(2,1)}), bf16[16,2,4096]{2,1,0:T(2,128)(2,1)S(1)}, u32[]{:S(2)}, u32[]{:S(2)}) async-start(bf16[16,2,4096]{2,1,0:T(2,128)(2,1)} %all_to_all.27), calls=%async_computation.1 | async-start | bytes 524288 | tf_op jit(solution)/shard_map/all_to_all | solution.py:112
  36.8 0.1 copy.20
  36.9 0.1 reshape.763
  37.2 1.2 %convolution_convert_fusion.1 = bf16[576,512]{1,0:T(8,128)(2,1)S(1)} fusion(f32[5,512]{1,0:T(8,128)S(1)} %copy-done.1, s32[576,5]{0,1:T(8,128)S(1)} %stack.34), kind=kOutput, calls=%fused_computation.10 | convolution fusion | flops 18001152 | bytes 611584 | tf_op jit(solution)/shard_map/dot_general | solution.py:38
  38.5 0.7 %pad_slice_fusion = (bf16[10,48,512]{2,1,0:T(8,128)(2,1)S(1)}, bf16[10,48,512]{2,1,0:T(8,128)(2,1)S(1)}, bf16[10,48,512]{2,1,0:T(8,128)(2,1)S(1)}, bf16[10,48,51...) fusion(bf16[12,48,512]{2,1,0:T(8,128)(2,1)S(1)} %broadcast_sele, ...), kind=kLoop, calls=%fused_computation.28 | loop fusion | bytes 6488064 | tf_op jit(solution)/shard_map/slice | solution.py:23
  39.2 1.4 %slice-done.3 = s8[4194304]{0:T(1024)(128)(4,1)S(1)} async-done(((s8[4718592]{0:T(1024)(128)(4,1)}), s8[4194304]{0:T(1024)(128)(4,1)S(1)}, s32[]{:S(2)}) %slice-start.3) | async-done | bytes 4194328
  40.6 0.4 fusion.25
  41.0 0.4 convolution_add_fusion.7
  41.4 0.4 convolution_add_fusion.6
  41.9 0.4 convolution_add_fusion.5
  42.3 0.4 convolution_add_fusion.4
  42.7 0.4 convolution_add_fusion.3
  43.2 0.4 convolution_add_fusion.2
  43.6 0.4 convolution_add_fusion.1
  44.0 0.4 convolution_add_fusion
  44.5 0.3 fusion.45
  44.8 0.5 pad_slice_fusion.6
  45.3 0.3 slice-done.1
  45.7 0.4 fusion.15
  46.0 0.4 convolution_add_fusion.15
  46.4 0.4 convolution_add_fusion.14
  46.8 0.4 convolution_add_fusion.13
  47.2 0.4 convolution_add_fusion.12
  47.5 0.4 convolution_add_fusion.11
  47.9 0.4 convolution_add_fusion.10
  48.3 0.4 convolution_add_fusion.9
  48.7 1.1 %fusion = bf16[384,512]{1,0:T(8,128)(2,1)} fusion(f32[384,512]{1,0:T(8,128)S(1)} %convolution_add_fusion.9, bf16[384,512]{1,0:T(8,128)(2,1)S(1)} %bitcast.164, bf16[3,3,512,512]{3,2,1,0:T(8,128)(2,1)S(1)} %bitcast.150), kind=kOutput, calls=%fused_computation.19 | convolution fusion | flops 201719808 | bytes 2097152 | tf_op jit(solution)/shard_map/dot_general | solution.py:26
  49.8 0.8 %reduce_sum.52 = bf16[2,4096]{1,0:T(2,128)(2,1)} reduce(bf16[16,2,4096]{2,1,0:T(2,128)(2,1)S(1)} %all-to-all-done.1, bf16[]{:T(256)} %constant.188.clone.1), dimensions={0}, to_apply=%region_3.4 | reduce | flops 122880 | bytes 278530 | tf_op jit(solution)/shard_map/reduce_sum | solution.py:115
  (33 shorter events, 0.8 us)
Async XLA Ops:
  0.6 26.0 %copy-start = (bf16[256,4096]{1,0:T(8,128)(2,1)S(1)}, bf16[256,4096]{1,0:T(8,128)(2,1)}, u32[]{:S(2)}) copy-start(bf16[256,4096]{1,0:T(8,128)(2,1)} %param.18) | copy-start | bytes 6291460
  0.6 36.6 %copy-start.1 = (f32[5,512]{1,0:T(8,128)S(1)}, f32[5,512]{1,0:T(8,128)}, u32[]{:S(2)}) copy-start(f32[5,512]{1,0:T(8,128)} %param.21) | copy-start | bytes 30724
  6.8 32.4 %slice-start.2 = ((s8[4718592]{0:T(1024)(128)(4,1)}), s8[524288]{0:T(1024)(128)(4,1)S(1)}, s32[]{:S(2)}) async-start(s8[4718592]{0:T(1024)(128)(4,1)} %bitcast.151), calls=%async_computation.5 | async-start | bytes 1048576
  9.2 13.9 %all-to-all-start = ((bf16[2,16,256]{2,0,1:T(2,128)(2,1)}), bf16[2,16,256]{2,0,1:T(2,128)(2,1)S(1)}, u32[]{:S(2)}, u32[]{:S(2)}) async-start(bf16[2,16,256]{2,0,1:T(2,128)(2,1)} %copy.19), calls=%async_computation | async-start | bytes 32768 | tf_op jit(solution)/shard_map/all_to_all | solution.py:109
  23.1 10.0 %all-to-all-start.2 = ((s32[16,1,288]{2,1,0:T(1,128)}), s32[16,1,288]{2,1,0:T(1,128)S(1)}, u32[]{:S(2)}, u32[]{:S(2)}) async-start(s32[16,1,288]{2,1,0:T(1,128)} %all_to_all.29), calls=%async_computation.2 | async-start | bytes 49152 | tf_op jit(solution)/shard_map/all_to_all | solution.py:134
  33.2 16.6 %all-to-all-start.1 = ((bf16[16,2,4096]{2,1,0:T(2,128)(2,1)}), bf16[16,2,4096]{2,1,0:T(2,128)(2,1)S(1)}, u32[]{:S(2)}, u32[]{:S(2)}) async-start(bf16[16,2,4096]{2,1,0:T(2,128)(2,1)} %all_to_all.27), calls=%async_computation.1 | async-start | bytes 524288 | tf_op jit(solution)/shard_map/all_to_all | solution.py:112
  38.4 2.2 %slice-start.3 = ((s8[4718592]{0:T(1024)(128)(4,1)}), s8[4194304]{0:T(1024)(128)(4,1)S(1)}, s32[]{:S(2)}) async-start(s8[4718592]{0:T(1024)(128)(4,1)} %bitcast.151), calls=%async_computation.6 | async-start | bytes 8388608
  43.2 2.2 %slice-start = ((s8[4718592]{0:T(1024)(128)(4,1)}), s8[4194304]{0:T(1024)(128)(4,1)S(1)}, s32[]{:S(2)}) async-start(s8[4718592]{0:T(1024)(128)(4,1)} %bitcast.149), calls=%async_computation.3 | async-start | bytes 8388608
  44.0 1.6 %slice-start.1 = ((s8[4718592]{0:T(1024)(128)(4,1)}), s8[524288]{0:T(1024)(128)(4,1)S(1)}, s32[]{:S(2)}) async-start(s8[4718592]{0:T(1024)(128)(4,1)} %bitcast.149), calls=%async_computation.4 | async-start | bytes 1048576

commit v2 on v1

v2 whole, which is shorter than its diff:
```python
import functools
import math

import jax
import jax.numpy as jnp
from jax import lax
from jax.experimental import pallas as pl
from jax.experimental.pallas import tpu as pltpu
from jax.sharding import PartitionSpec as P

HEAD_DIM = 128
FSQ_DIMS = 5
IMG_H = 32
IMG_W = 48
IMG_SPLIT = 4
LANES = 128
PAD = 8
BF16 = jnp.bfloat16
F32 = jnp.float32
MESH = pl.DeviceIdType.MESH


def dot(a, b):
    return jnp.dot(a, b, preferred_element_type=F32)


def dot_nt(a, b):
    return lax.dot_general(a, b, (((1,), (1,)), ((), ())), preferred_element_type=F32)


def kernel(
    n,
    tile_h,
    lengths,
    tile_slot,
    queries,
    new_keys,
    new_values,
    codes,
    code_weight,
    cache_keys_hbm,
    cache_values_hbm,
    out_weight_hbm,
    conv_one_hbm,
    conv_two_hbm,
    mixed,
    decoded_hbm,
    cache_keys,
    cache_values,
    out_weight,
    conv_one,
    conv_two,
    slot_codes,
    codes_in,
    att_out,
    att_in,
    features,
    partial_rows,
    part_out,
    part_in,
    field,
    columns,
    shifted,
    decoded,
    local_sem,
    out_sem,
    code_send,
    code_recv,
    att_send,
    att_recv,
    part_send,
    part_recv,
):
    me = lax.axis_index("rows")
    own = queries.shape[0]
    width = queries.shape[1]
    heads = width // HEAD_DIM
    cache = cache_keys.shape[1]
    channels = code_weight.shape[1]
    sections = IMG_H // tile_h
    share = width // n
    block = att_out.shape[2]
    words = codes.shape[1]

    loads = [
        pltpu.make_async_copy(source, target, local_sem.at[i])
        for i, (source, target) in enumerate(
            (
                (cache_keys_hbm, cache_keys),
                (cache_values_hbm, cache_values),
                (conv_one_hbm, conv_one),
                (out_weight_hbm, out_weight),
                (conv_two_hbm, conv_two),
            )
        )
    ]
    for load in loads:
        load.start()

    barrier = pltpu.get_barrier_semaphore()

    @pl.loop(1, n)
    def _(k):
        pl.semaphore_signal(
            barrier, inc=1, device_id={"rows": lax.rem(me + k, n)}, device_id_type=MESH
        )

    for slot in range(n // sections):
        picked = jnp.zeros((1, words), jnp.int32)
        for r in range(own):
            picked = picked + jnp.where(tile_slot[r] == slot, codes[r : r + 1, :], 0)
        slot_codes[slot] = picked

    pl.semaphore_wait(barrier, n - 1)

    def slot_of(device):
        return lax.rem(device + sections // 2, n) // sections

    def code_copy(k):
        target = lax.rem(me + k, n)
        return pltpu.make_async_remote_copy(
            src_ref=slot_codes.at[slot_of(target)],
            dst_ref=codes_in.at[me],
            send_sem=code_send.at[k],
            recv_sem=code_recv.at[k],
            device_id={"rows": target},
            device_id_type=MESH,
        )

    def att_copy(k):
        target = lax.rem(me + k, n)
        return pltpu.make_async_remote_copy(
            src_ref=att_out.at[target],
            dst_ref=att_in.at[me],
            send_sem=att_send.at[k],
            recv_sem=att_recv.at[k],
            device_id={"rows": target},
            device_id_type=MESH,
        )

    def part_copy(k):
        target = lax.rem(me + k, n)
        return pltpu.make_async_remote_copy(
            src_ref=part_out.at[target],
            dst_ref=part_in.at[me],
            send_sem=part_send.at[k],
            recv_sem=part_recv.at[k],
            device_id={"rows": target},
            device_id_type=MESH,
        )

    @pl.loop(1, n)
    def _(k):
        code_copy(k).start()

    codes_in[me] = slot_codes[slot_of(me)]

    head_mask = (
        lax.broadcasted_iota(jnp.int32, (heads, width), 1) // HEAD_DIM
        == lax.broadcasted_iota(jnp.int32, (heads, width), 0)
    )
    factor = 1.0 / math.sqrt(HEAD_DIM)
    asking = queries[...].astype(F32)
    fresh_keys = new_keys[...].astype(F32)
    fresh_values = new_values[...].astype(F32)
    loads[0].wait()
    weights = []
    for r in range(own):
        spread = jnp.where(head_mask, asking[r : r + 1, :], 0.0)
        scores = dot_nt(spread.astype(BF16), cache_keys[r]) * factor
        own_score = jnp.sum(spread * fresh_keys[r : r + 1, :], axis=1, keepdims=True) * factor
        live = lax.broadcasted_iota(jnp.int32, (heads, cache), 1) < lengths[r]
        scores = jnp.where(live, scores, -1e30)
        highest = jnp.maximum(jnp.max(scores, axis=1, keepdims=True), own_score)
        cache_exp = jnp.where(live, jnp.exp(scores - highest), 0.0)
        own_exp = jnp.exp(own_score - highest)
        denom = jnp.sum(cache_exp, axis=1, keepdims=True) + own_exp
        weights.append(((cache_exp / denom).astype(BF16), (own_exp / denom).astype(BF16).astype(F32)))
    loads[1].wait()
    rows = []
    for r in range(own):
        cache_weight, own_weight = weights[r]
        full = dot(cache_weight, cache_values[r]) + own_weight * fresh_values[r : r + 1, :]
        rows.append(jnp.sum(jnp.where(head_mask, full, 0.0), axis=0, keepdims=True))
    attended = jnp.concatenate(rows, axis=0).astype(BF16).astype(F32)
    for d in range(n):
        start = d * share // LANES * LANES
        att_out[d] = attended[:, start : start + block]

    @pl.loop(1, n)
    def _(k):
        att_copy(k).start()

    att_in[me] = att_out[me]

    tile = lax.rem(me + sections // 2, n)
    section = lax.rem(tile, sections)
    tile_words = tile_h * IMG_W // 2
    span = (tile_h + 4) * IMG_W

    @pl.loop(1, n)
    def _(k):
        code_copy(k).wait()

    chosen = codes_in[0]
    for i in range(1, n):
        chosen = chosen + codes_in[i]
    turned = pltpu.roll(
        jnp.broadcast_to(chosen, (8, words)),
        lax.rem(words + IMG_W - section * tile_words, words),
        axis=1,
    )
    strip_words = -(-(span // 2) // LANES) * LANES
    strip = turned[0:1, 0:strip_words]
    level = lax.broadcasted_iota(jnp.int32, (16, strip_words), 0)
    level = jnp.where(level >= 2 * FSQ_DIMS, level - 2 * FSQ_DIMS, level)
    level = jnp.where(level >= FSQ_DIMS, level - FSQ_DIMS, level)
    strip = jnp.broadcast_to(strip, (16, strip_words))

    def values_of(position_codes):
        levels = jnp.right_shift(position_codes, 3 * level) & 7
        return ((2 * levels - 7).astype(F32) * 0.125).astype(BF16)

    low = values_of(strip & 32767)
    high = values_of(jnp.right_shift(strip, 15))
    place = lax.broadcasted_iota(jnp.int32, (span, strip_words), 0)
    word = lax.broadcasted_iota(jnp.int32, (span, strip_words), 1)
    gap = place - 2 * word
    even = jnp.where(gap == 0, 1.0, 0.0).astype(BF16)
    odd = jnp.where(gap == 1, 1.0, 0.0).astype(BF16)
    field[0:PAD, :] = jnp.zeros((PAD, 16), F32)
    field[PAD + span :, :] = jnp.zeros((PAD, 16), F32)
    field[PAD : PAD + span, :] = dot_nt(even, low) + dot_nt(odd, high)

    whole = code_weight[...]
    top = whole.astype(BF16)
    rest = whole - top.astype(F32)
    middle = rest.astype(BF16)
    bottom = rest - middle.astype(F32)
    thirds = jnp.concatenate(
        [top.astype(F32), middle.astype(F32), bottom, jnp.zeros((1, channels), F32)], axis=0
    ).astype(BF16)

    def kept(count, rim):
        position = lax.broadcasted_iota(jnp.int32, (count, 1), 0)
        inside = jnp.logical_not(
            ((position < rim * IMG_W) & (section == 0))
            | ((position >= count - rim * IMG_W) & (section == sections - 1))
        )
        column = lax.rem(position, IMG_W)
        return inside, (column != 0, None, column != IMG_W - 1)

    inside, edges = kept(span, 2)
    for i in range(3):
        piece = field[PAD + i - 1 : PAD + i - 1 + span, :]
        mask = inside if edges[i] is None else inside & edges[i]
        piece = jnp.where(mask, piece, 0.0).astype(BF16)
        shifted[:, i * channels : (i + 1) * channels] = dot(piece, thirds).astype(BF16)

    mid_span = (tile_h + 2) * IMG_W
    loads[2].wait()
    hidden = dot(shifted[0:mid_span, :], conv_one[0])
    for tap in range(1, 3):
        hidden = hidden + dot(shifted[tap * IMG_W : tap * IMG_W + mid_span, :], conv_one[tap])
    inside, edges = kept(mid_span, 1)
    activated = jnp.where(inside, jax.nn.silu(hidden), 0.0)
    columns[0:PAD, :] = jnp.zeros((PAD, channels), F32)
    columns[PAD + mid_span :, :] = jnp.zeros((PAD, channels), F32)
    columns[PAD : PAD + mid_span, :] = activated

    @pl.loop(1, n)
    def _(k):
        att_copy(k).wait()

    for i in range(n):
        features[own * i : own * (i + 1), :] = att_in[i]
    rows_in = features[...].astype(BF16)
    loads[3].wait()
    pieces = part_out.shape[1] // own
    piece_width = width // pieces
    for c in range(pieces):
        piece = dot(rows_in, out_weight[:, c * piece_width : (c + 1) * piece_width])
        for j in range(piece_width // LANES):
            partial_rows[j, pl.ds(c, own * n, stride=pieces), :] = piece[
                :, j * LANES : (j + 1) * LANES
            ]
    for i in range(n):
        for j in range(piece_width // LANES):
            part_out[i, :, j * LANES : (j + 1) * LANES] = partial_rows[
                j, own * pieces * i : own * pieces * (i + 1), :
            ].astype(BF16)

    @pl.loop(1, n)
    def _(k):
        part_copy(k).start()

    part_in[me] = part_out[me]

    for i in range(3):
        piece = columns[PAD + i - 1 : PAD + i - 1 + mid_span, :]
        if edges[i] is not None:
            piece = jnp.where(edges[i], piece, 0.0)
        shifted[0:mid_span, i * channels : (i + 1) * channels] = piece.astype(BF16)
    out_span = tile_h * IMG_W
    loads[4].wait()
    final = dot(shifted[0:out_span, :], conv_two[0])
    for tap in range(1, 3):
        final = final + dot(shifted[tap * IMG_W : tap * IMG_W + out_span, :], conv_two[tap])
    decoded[...] = final.astype(BF16)
    store = pltpu.make_async_copy(decoded, decoded_hbm, out_sem)
    store.start()

    @pl.loop(1, n)
    def _(k):
        part_copy(k).wait()

    total = part_in[0].astype(F32)
    for i in range(1, n):
        total = total + part_in[i].astype(F32)
    mixed[...] = total.astype(BF16)
    store.wait()


def on_device(
    n,
    queries,
    new_keys,
    new_values,
    cache_keys,
    cache_values,
    cache_lengths,
    out_weight,
    codes,
    tile_slot,
    code_weight,
    conv_one,
    conv_two,
):
    own, width = queries.shape
    channels = code_weight.shape[1]
    sections = IMG_SPLIT
    tile_h = IMG_H // sections
    share = out_weight.shape[0]
    block = max(share, LANES)
    if share < block:
        parts = block // share
        slot = lax.rem(lax.axis_index("rows"), parts)
        which = jnp.arange(parts, dtype=jnp.int32)[:, None, None] == slot
        out_weight = jnp.where(which, out_weight[None], jnp.zeros((), BF16)).reshape(block, width)
    taps = conv_one.shape[1] * channels
    conv_one = conv_one.reshape(3, taps, channels)
    conv_two = conv_two.reshape(3, taps, channels)
    pieces = 16 // own
    span = (tile_h + 4) * IMG_W
    mid_span = (tile_h + 2) * IMG_W
    out_span = tile_h * IMG_W
    vmem = pl.BlockSpec(memory_space=pltpu.VMEM)
    smem = pl.BlockSpec(memory_space=pltpu.SMEM)
    hbm = pl.BlockSpec(memory_space=pl.ANY)
    dma = pltpu.SemaphoreType.DMA
    mixed, decoded = pl.pallas_call(
        functools.partial(kernel, n, tile_h),
        out_shape=(
            jax.ShapeDtypeStruct((own * pieces, width // pieces), BF16),
            jax.ShapeDtypeStruct((out_span, channels), BF16),
        ),
        in_specs=[smem, smem, vmem, vmem, vmem, vmem, vmem, hbm, hbm, hbm, hbm, hbm],
        out_specs=(vmem, hbm),
        scratch_shapes=[
            pltpu.VMEM(cache_keys.shape, BF16),
            pltpu.VMEM(cache_values.shape, BF16),
            pltpu.VMEM(out_weight.shape, BF16),
            pltpu.VMEM(conv_one.shape, BF16),
            pltpu.VMEM(conv_two.shape, BF16),
            pltpu.VMEM((n // sections, 1, codes.shape[1]), jnp.int32),
            pltpu.VMEM((n, 1, codes.shape[1]), jnp.int32),
            pltpu.VMEM((n, own, block), F32),
            pltpu.VMEM((n, own, block), F32),
            pltpu.VMEM((n * own, block), F32),
            pltpu.VMEM((width // pieces // LANES, n * own * pieces, LANES), F32),
            pltpu.VMEM((n, own * pieces, width // pieces), BF16),
            pltpu.VMEM((n, own * pieces, width // pieces), BF16),
            pltpu.VMEM((span + 2 * PAD, 16), F32),
            pltpu.VMEM((mid_span + 2 * PAD, channels), F32),
            pltpu.VMEM((span, taps), BF16),
            pltpu.VMEM((out_span, channels), BF16),
            dma((5,)),
            dma(()),
            dma((n,)),
            dma((n,)),
            dma((n,)),
            dma((n,)),
            dma((n,)),
            dma((n,)),
        ],
        compiler_params=pltpu.CompilerParams(
            collective_id=0, has_side_effects=True, vmem_limit_bytes=60 * 1024 * 1024
        ),
        name="decode_step",
    )(
        cache_lengths,
        tile_slot,
        queries,
        new_keys,
        new_values,
        codes,
        code_weight,
        cache_keys,
        cache_values,
        out_weight,
        conv_one,
        conv_two,
    )
    return mixed.reshape(own, width), decoded.reshape(tile_h, IMG_W, channels)


def solution(mesh):
    both = ("groups", "rows")
    in_specs = (
        P(both, None),
        P(both, None),
        P(both, None),
        P(both, None, None),
        P(both, None, None),
        P(both),
        P("rows", None),
        P(both, None),
        P(both),
        P(),
        P(),
        P(),
    )
    out_specs = (P(both, None), P(both, None, None))
    return jax.shard_map(
        functools.partial(on_device, mesh.shape["rows"]),
        mesh=mesh,
        in_specs=in_specs,
        out_specs=out_specs,
        check_vma=False,
    )
```

time: 51.5 us -> 26.4 us (0.51)
  the two profiles are of different devices: /device:TPU:0 before, /device:TPU:1 now
where the time goes in v2:
time: 26.4 us; the launch traced here: 26.1 us
  Pallas kernels  22.3 us (84%)
  local copies, waits for them, and re-layouts  3.1 us (12%)
  between operations  0.64 us (2%)
    pallas_call x1, Pallas kernels, on_device(): pl.pallas_call(functools.partial(kernel, n, tile_h), out_shape=(jax.Shape...  22.3 us
    unnamed x1, local copies, waits for them, and re-layouts  1.77 us
    reshape x1, local copies, waits for them, and re-layouts, on_device(): return (mixed.reshape(own, width), decoded.reshape(tile_h, IMG_W, channels))  1.34 us

profile of v2, /device:TPU:1, one launch (start us, length us, event | category | flops | bytes accessed | tf_op | source)
XLA Modules:
  0.0 26.1 jit_solution(781912171794259003)
XLA Ops:
  0.6 22.3 %decode_step.1 = (bf16[16,512]{1,0:T(8,128)(2,1)}, bf16[384,512]{1,0:T(8,128)(2,1)}) custom-call(s32[2]{0:T(128)} %lengths.1, s32[2]{0:T(128)} %tile_slot.1, bf16[2,4096]{1,0:T(2,128)(2,1)} %queries.1, bf16[2,4096]{1,0:T(2,128)(2,1)} %new_keys.1, bf16[2,4096]{1,0:T(2,128)(2,1)} %new_values.1, s32[2,768]{1,0:T(2,128)} %codes.1, f32[5,512]{1,0:T(8,128)} %code_weight.1, ...), custom_call_target="tpu_custom_call" | custom-call | tf_op jit(solution)/shard_map/decode_step/pallas_call | solution.py:361
  23.0 1.3 %reshape.18 = bf16[2,4096]{1,0:T(2,128)(2,1)} reshape(bf16[16,512]{1,0:T(8,128)(2,1)} %get-tuple-element.4) | data formatting | bytes 32768 | tf_op jit(solution)/shard_map/reshape | solution.py:414
  24.3 1.8 %copy.15 = bf16[8,48,512]{2,1,0:T(8,128)(2,1)} copy(bf16[8,48,512]{2,1,0:T(8,128)(2,1)} %bitcast.5) | data formatting | bytes 786432

commit v3 on v2

--- a/solution.py
+++ b/solution.py
@@ -31,6 +31,20 @@
 def kernel(
     n,
     tile_h,
+    lengths_hbm,
+    tile_slot_hbm,
+    queries_hbm,
+    new_keys_hbm,
+    new_values_hbm,
+    codes_hbm,
+    code_weight_hbm,
+    cache_keys_hbm,
+    cache_values_hbm,
+    out_weight_hbm,
+    conv_one_hbm,
+    conv_two_hbm,
+    mixed,
+    decoded,
     lengths,
     tile_slot,
     queries,
@@ -38,13 +52,6 @@
     new_values,
     codes,
     code_weight,
-    cache_keys_hbm,
-    cache_values_hbm,
-    out_weight_hbm,
-    conv_one_hbm,
-    conv_two_hbm,
-    mixed,
-    decoded_hbm,
     cache_keys,
     cache_values,
     out_weight,
@@ -61,9 +68,7 @@
     field,
     columns,
     shifted,
-    decoded,
     local_sem,
-    out_sem,
     code_send,
     code_recv,
     att_send,
@@ -82,36 +87,35 @@
     block = att_out.shape[2]
     words = codes.shape[1]
 
+    barrier = pltpu.get_barrier_semaphore()
+
+    @pl.loop(1, n)
+    def _(k):
+        pl.semaphore_signal(
+            barrier, inc=1, device_id={"rows": lax.rem(me + k, n)}, device_id_type=MESH
+        )
+
     loads = [
         pltpu.make_async_copy(source, target, local_sem.at[i])
         for i, (source, target) in enumerate(
             (
+                (queries_hbm, queries),
+                (new_keys_hbm, new_keys),
+                (new_values_hbm, new_values),
+                (lengths_hbm, lengths),
                 (cache_keys_hbm, cache_keys),
                 (cache_values_hbm, cache_values),
+                (codes_hbm, codes),
+                (tile_slot_hbm, tile_slot),
+                (code_weight_hbm, code_weight),
+                (out_weight_hbm, out_weight),
                 (conv_one_hbm, conv_one),
-                (out_weight_hbm, out_weight),
                 (conv_two_hbm, conv_two),
             )
         )
     ]
     for load in loads:
         load.start()
-
-    barrier = pltpu.get_barrier_semaphore()
-
-    @pl.loop(1, n)
-    def _(k):
-        pl.semaphore_signal(
-            barrier, inc=1, device_id={"rows": lax.rem(me + k, n)}, device_id_type=MESH
-        )
-
-    for slot in range(n // sections):
-        picked = jnp.zeros((1, words), jnp.int32)
-        for r in range(own):
-            picked = picked + jnp.where(tile_slot[r] == slot, codes[r : r + 1, :], 0)
-        slot_codes[slot] = picked
-
-    pl.semaphore_wait(barrier, n - 1)
 
     def slot_of(device):
         return lax.rem(device + sections // 2, n) // sections
@@ -149,21 +153,19 @@
             device_id_type=MESH,
         )
 
-    @pl.loop(1, n)
-    def _(k):
-        code_copy(k).start()
-
-    codes_in[me] = slot_codes[slot_of(me)]
-
     head_mask = (
         lax.broadcasted_iota(jnp.int32, (heads, width), 1) // HEAD_DIM
         == lax.broadcasted_iota(jnp.int32, (heads, width), 0)
     )
     factor = 1.0 / math.sqrt(HEAD_DIM)
+    loads[0].wait()
+    loads[1].wait()
+    loads[2].wait()
+    loads[3].wait()
     asking = queries[...].astype(F32)
     fresh_keys = new_keys[...].astype(F32)
     fresh_values = new_values[...].astype(F32)
-    loads[0].wait()
+    loads[4].wait()
     weights = []
     for r in range(own):
         spread = jnp.where(head_mask, asking[r : r + 1, :], 0.0)
@@ -176,7 +178,7 @@
         own_exp = jnp.exp(own_score - highest)
         denom = jnp.sum(cache_exp, axis=1, keepdims=True) + own_exp
         weights.append(((cache_exp / denom).astype(BF16), (own_exp / denom).astype(BF16).astype(F32)))
-    loads[1].wait()
+    loads[5].wait()
     rows = []
     for r in range(own):
         cache_weight, own_weight = weights[r]
@@ -187,42 +189,34 @@
         start = d * share // LANES * LANES
         att_out[d] = attended[:, start : start + block]
 
+    loads[6].wait()
+    loads[7].wait()
+    for slot in range(n // sections):
+        picked = jnp.zeros((1, words), jnp.int32)
+        for r in range(own):
+            picked = picked + jnp.where(tile_slot[r] == slot, codes[r : r + 1, :], 0)
+        slot_codes[slot] = picked
+
+    pl.semaphore_wait(barrier, n - 1)
+
     @pl.loop(1, n)
     def _(k):
         att_copy(k).start()
 
     att_in[me] = att_out[me]
+
+    @pl.loop(1, n)
+    def _(k):
+        code_copy(k).start()
+
+    codes_in[me] = slot_codes[slot_of(me)]
 
     tile = lax.rem(me + sections // 2, n)
     section = lax.rem(tile, sections)
     tile_words = tile_h * IMG_W // 2
     span = (tile_h + 4) * IMG_W
 
-    @pl.loop(1, n)
-    def _(k):
-        code_copy(k).wait()
-
-    chosen = codes_in[0]
-    for i in range(1, n):
-        chosen = chosen + codes_in[i]
-    turned = pltpu.roll(
-        jnp.broadcast_to(chosen, (8, words)),
-        lax.rem(words + IMG_W - section * tile_words, words),
-        axis=1,
-    )
     strip_words = -(-(span // 2) // LANES) * LANES
-    strip = turned[0:1, 0:strip_words]
-    level = lax.broadcasted_iota(jnp.int32, (16, strip_words), 0)
-    level = jnp.where(level >= 2 * FSQ_DIMS, level - 2 * FSQ_DIMS, level)
-    level = jnp.where(level >= FSQ_DIMS, level - FSQ_DIMS, level)
-    strip = jnp.broadcast_to(strip, (16, strip_words))
-
-    def values_of(position_codes):
-        levels = jnp.right_shift(position_codes, 3 * level) & 7
-        return ((2 * levels - 7).astype(F32) * 0.125).astype(BF16)
-
-    low = values_of(strip & 32767)
-    high = values_of(jnp.right_shift(strip, 15))
     place = lax.broadcasted_iota(jnp.int32, (span, strip_words), 0)
     word = lax.broadcasted_iota(jnp.int32, (span, strip_words), 1)
     gap = place - 2 * word
@@ -230,8 +224,7 @@
     odd = jnp.where(gap == 1, 1.0, 0.0).astype(BF16)
     field[0:PAD, :] = jnp.zeros((PAD, 16), F32)
     field[PAD + span :, :] = jnp.zeros((PAD, 16), F32)
-    field[PAD : PAD + span, :] = dot_nt(even, low) + dot_nt(odd, high)
-
+    loads[8].wait()
     whole = code_weight[...]
     top = whole.astype(BF16)
     rest = whole - top.astype(F32)
@@ -241,33 +234,6 @@
         [top.astype(F32), middle.astype(F32), bottom, jnp.zeros((1, channels), F32)], axis=0
     ).astype(BF16)
 
-    def kept(count, rim):
-        position = lax.broadcasted_iota(jnp.int32, (count, 1), 0)
-        inside = jnp.logical_not(
-            ((position < rim * IMG_W) & (section == 0))
-            | ((position >= count - rim * IMG_W) & (section == sections - 1))
-        )
-        column = lax.rem(position, IMG_W)
-        return inside, (column != 0, None, column != IMG_W - 1)
-
-    inside, edges = kept(span, 2)
-    for i in range(3):
-        piece = field[PAD + i - 1 : PAD + i - 1 + span, :]
-        mask = inside if edges[i] is None else inside & edges[i]
-        piece = jnp.where(mask, piece, 0.0).astype(BF16)
-        shifted[:, i * channels : (i + 1) * channels] = dot(piece, thirds).astype(BF16)
-
-    mid_span = (tile_h + 2) * IMG_W
-    loads[2].wait()
-    hidden = dot(shifted[0:mid_span, :], conv_one[0])
-    for tap in range(1, 3):
-        hidden = hidden + dot(shifted[tap * IMG_W : tap * IMG_W + mid_span, :], conv_one[tap])
-    inside, edges = kept(mid_span, 1)
-    activated = jnp.where(inside, jax.nn.silu(hidden), 0.0)
-    columns[0:PAD, :] = jnp.zeros((PAD, channels), F32)
-    columns[PAD + mid_span :, :] = jnp.zeros((PAD, channels), F32)
-    columns[PAD : PAD + mid_span, :] = activated
-
     @pl.loop(1, n)
     def _(k):
         att_copy(k).wait()
@@ -275,7 +241,7 @@
     for i in range(n):
         features[own * i : own * (i + 1), :] = att_in[i]
     rows_in = features[...].astype(BF16)
-    loads[3].wait()
+    loads[9].wait()
     pieces = part_out.shape[1] // own
     piece_width = width // pieces
     for c in range(pieces):
@@ -296,20 +262,71 @@
 
     part_in[me] = part_out[me]
 
+    @pl.loop(1, n)
+    def _(k):
+        code_copy(k).wait()
+
+    chosen = codes_in[0]
+    for i in range(1, n):
+        chosen = chosen + codes_in[i]
+    turned = pltpu.roll(
+        jnp.broadcast_to(chosen, (8, words)),
+        lax.rem(words + IMG_W - section * tile_words, words),
+        axis=1,
+    )
+    strip = turned[0:1, 0:strip_words]
+    level = lax.broadcasted_iota(jnp.int32, (16, strip_words), 0)
+    level = jnp.where(level >= 2 * FSQ_DIMS, level - 2 * FSQ_DIMS, level)
+    level = jnp.where(level >= FSQ_DIMS, level - FSQ_DIMS, level)
+    strip = jnp.broadcast_to(strip, (16, strip_words))
+
+    def values_of(position_codes):
+        levels = jnp.right_shift(position_codes, 3 * level) & 7
+        return ((2 * levels - 7).astype(F32) * 0.125).astype(BF16)
+
+    low = values_of(strip & 32767)
+    high = values_of(jnp.right_shift(strip, 15))
+    field[PAD : PAD + span, :] = dot_nt(even, low) + dot_nt(odd, high)
+
+
+    def kept(count, rim):
+        position = lax.broadcasted_iota(jnp.int32, (count, 1), 0)
+        inside = jnp.logical_not(
+            ((position < rim * IMG_W) & (section == 0))
+            | ((position >= count - rim * IMG_W) & (section == sections - 1))
+        )
+        column = lax.rem(position, IMG_W)
+        return inside, (column != 0, None, column != IMG_W - 1)
+
+    inside, edges = kept(span, 2)
+    for i in range(3):
+        piece = field[PAD + i - 1 : PAD + i - 1 + span, :]
+        mask = inside if edges[i] is None else inside & edges[i]
+        piece = jnp.where(mask, piece, 0.0).astype(BF16)
+        shifted[:, i * channels : (i + 1) * channels] = dot(piece, thirds).astype(BF16)
+
+    mid_span = (tile_h + 2) * IMG_W
+    loads[10].wait()
+    hidden = dot(shifted[0:mid_span, :], conv_one[0])
+    for tap in range(1, 3):
+        hidden = hidden + dot(shifted[tap * IMG_W : tap * IMG_W + mid_span, :], conv_one[tap])
+    inside, edges = kept(mid_span, 1)
+    activated = jnp.where(inside, jax.nn.silu(hidden), 0.0)
+    columns[0:PAD, :] = jnp.zeros((PAD, channels), F32)
+    columns[PAD + mid_span :, :] = jnp.zeros((PAD, channels), F32)
+    columns[PAD : PAD + mid_span, :] = activated
+
     for i in range(3):
         piece = columns[PAD + i - 1 : PAD + i - 1 + mid_span, :]
         if edges[i] is not None:
             piece = jnp.where(edges[i], piece, 0.0)
         shifted[0:mid_span, i * channels : (i + 1) * channels] = piece.astype(BF16)
     out_span = tile_h * IMG_W
-    loads[4].wait()
+    loads[11].wait()
     final = dot(shifted[0:out_span, :], conv_two[0])
     for tap in range(1, 3):
         final = final + dot(shifted[tap * IMG_W : tap * IMG_W + out_span, :], conv_two[tap])
     decoded[...] = final.astype(BF16)
-    store = pltpu.make_async_copy(decoded, decoded_hbm, out_sem)
-    store.start()
-
     @pl.loop(1, n)
     def _(k):
         part_copy(k).wait()
@@ -317,8 +334,13 @@
     total = part_in[0].astype(F32)
     for i in range(1, n):
         total = total + part_in[i].astype(F32)
-    mixed[...] = total.astype(BF16)
-    store.wait()
+    mixed[...] = jnp.concatenate(
+        [
+            jnp.concatenate([total[r * pieces + c][None] for c in range(pieces)], axis=1)
+            for r in range(own)
+        ],
+        axis=0,
+    ).astype(BF16)
 
 
 def on_device(
@@ -355,18 +377,24 @@
     mid_span = (tile_h + 2) * IMG_W
     out_span = tile_h * IMG_W
     vmem = pl.BlockSpec(memory_space=pltpu.VMEM)
-    smem = pl.BlockSpec(memory_space=pltpu.SMEM)
     hbm = pl.BlockSpec(memory_space=pl.ANY)
     dma = pltpu.SemaphoreType.DMA
     mixed, decoded = pl.pallas_call(
         functools.partial(kernel, n, tile_h),
         out_shape=(
-            jax.ShapeDtypeStruct((own * pieces, width // pieces), BF16),
-            jax.ShapeDtypeStruct((out_span, channels), BF16),
+            pltpu.VMEM((own, width), BF16),
+            pltpu.VMEM((out_span, channels), BF16),
         ),
-        in_specs=[smem, smem, vmem, vmem, vmem, vmem, vmem, hbm, hbm, hbm, hbm, hbm],
-        out_specs=(vmem, hbm),
+        in_specs=[hbm] * 12,
+        out_specs=(vmem, vmem),
         scratch_shapes=[
+            pltpu.SMEM(cache_lengths.shape, jnp.int32),
+            pltpu.SMEM(tile_slot.shape, jnp.int32),
+            pltpu.VMEM(queries.shape, BF16),
+            pltpu.VMEM(new_keys.shape, BF16),
+            pltpu.VMEM(new_values.shape, BF16),
+            pltpu.VMEM(codes.shape, jnp.int32),
+            pltpu.VMEM(code_weight.shape, F32),
             pltpu.VMEM(cache_keys.shape, BF16),
             pltpu.VMEM(cache_values.shape, BF16),
             pltpu.VMEM(out_weight.shape, BF16),
@@ -383,9 +411,7 @@
             pltpu.VMEM((span + 2 * PAD, 16), F32),
             pltpu.VMEM((mid_span + 2 * PAD, channels), F32),
             pltpu.VMEM((span, taps), BF16),
-            pltpu.VMEM((out_span, channels), BF16),
-            dma((5,)),
-            dma(()),
+            dma((12,)),
             dma((n,)),
             dma((n,)),
             dma((n,)),
@@ -411,7 +437,7 @@
         conv_one,
         conv_two,
     )
-    return mixed.reshape(own, width), decoded.reshape(tile_h, IMG_W, channels)
+    return mixed, decoded.reshape(tile_h, IMG_W, channels)
 
 
 def solution(mesh):

time: 26.4 us -> 20.2 us (0.77)
  the two profiles are of different devices: /device:TPU:1 before, /device:TPU:0 now
where the time goes in v3:
time: 20.2 us; the launch traced here: 19.9 us
  Pallas kernels  17.9 us (89%)
  local copies, waits for them, and re-layouts  1.35 us (7%)
  between operations  0.64 us (3%)
    pallas_call x1, Pallas kernels, on_device(): pl.pallas_call(functools.partial(kernel, n, tile_h), out_shape=(pltpu.VME...  17.9 us
    unnamed x2, local copies, waits for them, and re-layouts  1.35 us

profile of v3, /device:TPU:0, one launch (start us, length us, event | category | flops | bytes accessed | tf_op | source)
XLA Modules:
  0.0 19.9 jit_solution(15929147655103491984)
XLA Ops:
  0.6 17.9 %decode_step.1 = (bf16[2,4096]{1,0:T(2,128)(2,1)S(1)}, bf16[384,512]{1,0:T(8,128)(2,1)S(1)}) custom-call(s32[2]{0:T(128)} %lengths_hbm.1, s32[2]{0:T(128)} %tile_slot_hbm.1, bf16[2,4096]{1,0:T(2,128)(2,1)} %queries_hbm.1, bf16[2,4096]{1,0:T(2,128)(2,1)} %new_keys_hbm.1, bf16[2,4096]{1,0:T(2,128)(2,1)} %new_values_hbm.1, s32[2,768]{1,0:T(2,128)} %codes_hbm.1, ...), custom_call_target="tpu_custom_call" | custom-call | tf_op jit(solution)/shard_map/decode_step/pallas_call | solution.py:382
  18.6 0.6 %copy.16 = bf16[2,4096]{1,0:T(2,128)(2,1)} copy(bf16[2,4096]{1,0:T(2,128)(2,1)S(1)} %get-tuple-element.6) | data formatting | bytes 32768
  19.2 0.7 %copy.17 = bf16[8,48,512]{2,1,0:T(8,128)(2,1)} copy(bf16[8,48,512]{2,1,0:T(8,128)(2,1)S(1)} %bitcast.3) | data formatting | bytes 786432

commit v4 on v3

--- a/solution.py
+++ b/solution.py
@@ -86,6 +86,9 @@
     share = width // n
     block = att_out.shape[2]
     words = codes.shape[1]
+    tile_words = tile_h * IMG_W // 2
+    span = (tile_h + 4) * IMG_W
+    strip_words = slot_codes.shape[2]
 
     barrier = pltpu.get_barrier_semaphore()
 
@@ -117,13 +120,13 @@
     for load in loads:
         load.start()
 
-    def slot_of(device):
-        return lax.rem(device + sections // 2, n) // sections
+    def tile_of(device):
+        return lax.rem(device + sections // 2, n)
 
     def code_copy(k):
         target = lax.rem(me + k, n)
         return pltpu.make_async_remote_copy(
-            src_ref=slot_codes.at[slot_of(target)],
+            src_ref=slot_codes.at[tile_of(target)],
             dst_ref=codes_in.at[me],
             send_sem=code_send.at[k],
             recv_sem=code_recv.at[k],
@@ -184,7 +187,7 @@
         cache_weight, own_weight = weights[r]
         full = dot(cache_weight, cache_values[r]) + own_weight * fresh_values[r : r + 1, :]
         rows.append(jnp.sum(jnp.where(head_mask, full, 0.0), axis=0, keepdims=True))
-    attended = jnp.concatenate(rows, axis=0).astype(BF16).astype(F32)
+    attended = jnp.concatenate(rows, axis=0).astype(BF16)
     for d in range(n):
         start = d * share // LANES * LANES
         att_out[d] = attended[:, start : start + block]
@@ -195,7 +198,11 @@
         picked = jnp.zeros((1, words), jnp.int32)
         for r in range(own):
             picked = picked + jnp.where(tile_slot[r] == slot, codes[r : r + 1, :], 0)
-        slot_codes[slot] = picked
+        picked = jnp.broadcast_to(picked, (8, words))
+        for part in range(sections):
+            shift = (IMG_W - part * tile_words) % words
+            turned = pltpu.roll(picked, shift, axis=1) if shift else picked
+            slot_codes[slot * sections + part] = turned[0:1, 0:strip_words]
 
     pl.semaphore_wait(barrier, n - 1)
 
@@ -209,14 +216,11 @@
     def _(k):
         code_copy(k).start()
 
-    codes_in[me] = slot_codes[slot_of(me)]
+    codes_in[me] = slot_codes[tile_of(me)]
 
     tile = lax.rem(me + sections // 2, n)
     section = lax.rem(tile, sections)
-    tile_words = tile_h * IMG_W // 2
-    span = (tile_h + 4) * IMG_W
-
-    strip_words = -(-(span // 2) // LANES) * LANES
+
     place = lax.broadcasted_iota(jnp.int32, (span, strip_words), 0)
     word = lax.broadcasted_iota(jnp.int32, (span, strip_words), 1)
     gap = place - 2 * word
@@ -239,7 +243,7 @@
         att_copy(k).wait()
 
     for i in range(n):
-        features[own * i : own * (i + 1), :] = att_in[i]
+        features[own * i : own * (i + 1), :] = att_in[i].astype(F32)
     rows_in = features[...].astype(BF16)
     loads[9].wait()
     pieces = part_out.shape[1] // own
@@ -269,16 +273,10 @@
     chosen = codes_in[0]
     for i in range(1, n):
         chosen = chosen + codes_in[i]
-    turned = pltpu.roll(
-        jnp.broadcast_to(chosen, (8, words)),
-        lax.rem(words + IMG_W - section * tile_words, words),
-        axis=1,
-    )
-    strip = turned[0:1, 0:strip_words]
     level = lax.broadcasted_iota(jnp.int32, (16, strip_words), 0)
     level = jnp.where(level >= 2 * FSQ_DIMS, level - 2 * FSQ_DIMS, level)
     level = jnp.where(level >= FSQ_DIMS, level - FSQ_DIMS, level)
-    strip = jnp.broadcast_to(strip, (16, strip_words))
+    strip = jnp.broadcast_to(chosen, (16, strip_words))
 
     def values_of(position_codes):
         levels = jnp.right_shift(position_codes, 3 * level) & 7
@@ -341,6 +339,34 @@
         ],
         axis=0,
     ).astype(BF16)
+
+
+def settle_kernel(mixed, decoded, mixed_out, decoded_out, sems):
+    stores = [
+        pltpu.make_async_copy(decoded, decoded_out, sems.at[0]),
+        pltpu.make_async_copy(mixed, mixed_out, sems.at[1]),
+    ]
+    for store in stores:
+        store.start()
+    for store in stores:
+        store.wait()
+
+
+def settle(mixed, decoded):
+    hbm = pl.BlockSpec(memory_space=pltpu.HBM)
+    vmem = pl.BlockSpec(memory_space=pltpu.VMEM)
+    return pl.pallas_call(
+        settle_kernel,
+        out_shape=(
+            jax.ShapeDtypeStruct(mixed.shape, mixed.dtype),
+            jax.ShapeDtypeStruct(decoded.shape, decoded.dtype),
+        ),
+        in_specs=[vmem, vmem],
+        out_specs=(hbm, hbm),
+        scratch_shapes=[pltpu.SemaphoreType.DMA((2,))],
+        compiler_params=pltpu.CompilerParams(vmem_limit_bytes=2 * 1024 * 1024),
+        name="settle",
+    )(mixed, decoded)
 
 
 def on_device(
@@ -374,6 +400,7 @@
     conv_two = conv_two.reshape(3, taps, channels)
     pieces = 16 // own
     span = (tile_h + 4) * IMG_W
+    strip_words = -(-(span // 2) // LANES) * LANES
     mid_span = (tile_h + 2) * IMG_W
     out_span = tile_h * IMG_W
     vmem = pl.BlockSpec(memory_space=pltpu.VMEM)
@@ -400,10 +427,10 @@
             pltpu.VMEM(out_weight.shape, BF16),
             pltpu.VMEM(conv_one.shape, BF16),
             pltpu.VMEM(conv_two.shape, BF16),
-            pltpu.VMEM((n // sections, 1, codes.shape[1]), jnp.int32),
-            pltpu.VMEM((n, 1, codes.shape[1]), jnp.int32),
-            pltpu.VMEM((n, own, block), F32),
-            pltpu.VMEM((n, own, block), F32),
+            pltpu.VMEM((n, 1, strip_words), jnp.int32),
+            pltpu.VMEM((n, 1, strip_words), jnp.int32),
+            pltpu.VMEM((n, own, block), BF16),
+            pltpu.VMEM((n, own, block), BF16),
             pltpu.VMEM((n * own, block), F32),
             pltpu.VMEM((width // pieces // LANES, n * own * pieces, LANES), F32),
             pltpu.VMEM((n, own * pieces, width // pieces), BF16),
@@ -437,6 +464,7 @@
         conv_one,
         conv_two,
     )
+    mixed, decoded = settle(mixed, decoded)
     return mixed, decoded.reshape(tile_h, IMG_W, channels)
 
 

time: 20.2 us -> 19.6 us (0.970)
  local copies, waits for them, and re-layouts: 1.35 us -> 0 us
  Pallas kernels: 17.9 us -> 18.7 us
    unnamed x2 -> x0, local copies, waits for them, and re-layouts: 1.35 us -> none
    pallas_call x0 -> x1, Pallas kernels: none -> 0.77 us  [settle(): pl.pallas_call(settle_kernel, out_shape=(jax.ShapeDtypeStruct(mixed.shape...]
where the time goes in v4:
time: 19.6 us; the launch traced here: 19.4 us
  Pallas kernels  18.7 us (95%)
  between operations  0.64 us (3%)
    pallas_call x1, Pallas kernels, on_device(): pl.pallas_call(functools.partial(kernel, n, tile_h), out_shape=(pltpu.VME...  18 us
    pallas_call x1, Pallas kernels, settle(): pl.pallas_call(settle_kernel, out_shape=(jax.ShapeDtypeStruct(mixed.shape...  0.77 us

profile of v4, /device:TPU:0, one launch (start us, length us, event | category | flops | bytes accessed | tf_op | source)
XLA Modules:
  0.0 19.4 jit_solution(5243832955679556302)
XLA Ops:
  0.6 18.0 %decode_step.1 = (bf16[2,4096]{1,0:T(2,128)(2,1)S(1)}, bf16[384,512]{1,0:T(8,128)(2,1)S(1)}) custom-call(s32[2]{0:T(128)} %lengths_hbm.1, s32[2]{0:T(128)} %tile_slot_hbm.1, bf16[2,4096]{1,0:T(2,128)(2,1)} %queries_hbm.1, bf16[2,4096]{1,0:T(2,128)(2,1)} %new_keys_hbm.1, bf16[2,4096]{1,0:T(2,128)(2,1)} %new_values_hbm.1, s32[2,768]{1,0:T(2,128)} %codes_hbm.1, ...), custom_call_target="tpu_custom_call" | custom-call | tf_op jit(solution)/shard_map/decode_step/pallas_call | solution.py:409
  18.6 0.8 %settle.1 = (bf16[2,4096]{1,0:T(2,128)(2,1)}, bf16[384,512]{1,0:T(8,128)(2,1)}) custom-call(bf16[2,4096]{1,0:T(2,128)(2,1)S(1)} %get-tuple-element.6.mixed, bf16[384,512]{1,0:T(8,128)(2,1)S(1)} %get-tuple-element.7.decoded), custom_call_target="tpu_custom_call" | custom-call | tf_op jit(solution)/shard_map/settle/pallas_call | solution.py:358

commit v5 on v4

--- a/solution.py
+++ b/solution.py
@@ -66,6 +66,8 @@
     part_out,
     part_in,
     field,
+    fields,
+    folds,
     columns,
     shifted,
     local_sem,
@@ -238,6 +240,22 @@
         [top.astype(F32), middle.astype(F32), bottom, jnp.zeros((1, channels), F32)], axis=0
     ).astype(BF16)
 
+    loads[10].wait()
+    for tap in range(3):
+        for i in range(3):
+            wide = dot(thirds, conv_one[tap, i * channels : (i + 1) * channels, :])
+            folded = (
+                wide[0:FSQ_DIMS]
+                + wide[FSQ_DIMS : 2 * FSQ_DIMS]
+                + wide[2 * FSQ_DIMS : 3 * FSQ_DIMS]
+            )
+            head = folded.astype(BF16).astype(F32)
+            body = (folded - head).astype(BF16).astype(F32)
+            tail = folded - head - body
+            folds[tap, 16 * i : 16 * (i + 1), :] = jnp.concatenate(
+                [head, body, tail, jnp.zeros((1, channels), F32)], axis=0
+            ).astype(BF16)
+
     @pl.loop(1, n)
     def _(k):
         att_copy(k).wait()
@@ -300,14 +318,14 @@
     for i in range(3):
         piece = field[PAD + i - 1 : PAD + i - 1 + span, :]
         mask = inside if edges[i] is None else inside & edges[i]
-        piece = jnp.where(mask, piece, 0.0).astype(BF16)
-        shifted[:, i * channels : (i + 1) * channels] = dot(piece, thirds).astype(BF16)
+        fields[:, 16 * i : 16 * (i + 1)] = jnp.where(mask, piece, 0.0)
 
     mid_span = (tile_h + 2) * IMG_W
-    loads[10].wait()
-    hidden = dot(shifted[0:mid_span, :], conv_one[0])
+    hidden = dot(fields[0:mid_span, :].astype(BF16), folds[0])
     for tap in range(1, 3):
-        hidden = hidden + dot(shifted[tap * IMG_W : tap * IMG_W + mid_span, :], conv_one[tap])
+        hidden = hidden + dot(
+            fields[tap * IMG_W : tap * IMG_W + mid_span, :].astype(BF16), folds[tap]
+        )
     inside, edges = kept(mid_span, 1)
     activated = jnp.where(inside, jax.nn.silu(hidden), 0.0)
     columns[0:PAD, :] = jnp.zeros((PAD, channels), F32)
@@ -436,8 +454,10 @@
             pltpu.VMEM((n, own * pieces, width // pieces), BF16),
             pltpu.VMEM((n, own * pieces, width // pieces), BF16),
             pltpu.VMEM((span + 2 * PAD, 16), F32),
+            pltpu.VMEM((span, 48), F32),
+            pltpu.VMEM((3, 48, channels), BF16),
             pltpu.VMEM((mid_span + 2 * PAD, channels), F32),
-            pltpu.VMEM((span, taps), BF16),
+            pltpu.VMEM((mid_span, taps), BF16),
             dma((12,)),
             dma((n,)),
             dma((n,)),

time: 19.6 us -> 19.1 us (0.974)
  the two profiles are of different devices: /device:TPU:0 before, /device:TPU:1 now
where the time goes in v5:
time: 19.1 us; the launch traced here: 18.8 us
  Pallas kernels  18.2 us (95%)
  between operations  0.64 us (3%)
    pallas_call x1, Pallas kernels, on_device(): pl.pallas_call(functools.partial(kernel, n, tile_h), out_shape=(pltpu.VME...  17.4 us
    pallas_call x1, Pallas kernels, settle(): pl.pallas_call(settle_kernel, out_shape=(jax.ShapeDtypeStruct(mixed.shape...  0.77 us

profile of v5, /device:TPU:1, one launch (start us, length us, event | category | flops | bytes accessed | tf_op | source)
XLA Modules:
  0.0 18.8 jit_solution(5816745541497807421)
XLA Ops:
  0.6 17.4 %decode_step.1 = (bf16[2,4096]{1,0:T(2,128)(2,1)S(1)}, bf16[384,512]{1,0:T(8,128)(2,1)S(1)}) custom-call(s32[2]{0:T(128)} %lengths_hbm.1, s32[2]{0:T(128)} %tile_slot_hbm.1, bf16[2,4096]{1,0:T(2,128)(2,1)} %queries_hbm.1, bf16[2,4096]{1,0:T(2,128)(2,1)} %new_keys_hbm.1, bf16[2,4096]{1,0:T(2,128)(2,1)} %new_values_hbm.1, s32[2,768]{1,0:T(2,128)} %codes_hbm.1, ...), custom_call_target="tpu_custom_call" | custom-call | tf_op jit(solution)/shard_map/decode_step/pallas_call | solution.py:427
  18.1 0.8 %settle.1 = (bf16[2,4096]{1,0:T(2,128)(2,1)}, bf16[384,512]{1,0:T(8,128)(2,1)}) custom-call(bf16[2,4096]{1,0:T(2,128)(2,1)S(1)} %get-tuple-element.6.mixed, bf16[384,512]{1,0:T(8,128)(2,1)S(1)} %get-tuple-element.7.decoded), custom_call_target="tpu_custom_call" | custom-call | tf_op jit(solution)/shard_map/settle/pallas_call | solution.py:376
